TPU v7x, 32 devices: a whole 2x2x4 slice. The times are simulated.
32 devices in a mesh: dp: 4 (over z), table: 8 (over y, x, core).
Axes of the slice: x: 2, y: 2, z: 4, core: 2. Of those that a mesh axis runs over, the one named last changes fastest.
Arguments:
- item_emb: bfloat16 [16384, 512], P(('dp', 'table')), may hold values from -6 to 6
- cotangent: bfloat16 [16384, 512], P(('dp', 'table')), may hold values from -6 to 6
- in_proj: bfloat16 [512, 2048], replicated, may hold values from -0.25 to 0.25
- out_proj: bfloat16 [512, 512], replicated, may hold values from -0.25 to 0.25
- history_lengths: int32 [32, 8], P(('dp', 'table')), may hold values from 1 to 256, 512 in all within a row
- item_ids: int32 [16384], P(('dp', 'table')), may hold values from 0 to 32767, as said below
Outputs:
- emb_grad: float32 [32768, 512], P(('dp', 'table'))
- in_grad: float32 [512, 2048], replicated
- out_grad: float32 [512, 512], replicated
Inputs may be any that keep to these rules, and one draw needn't show every extreme that they name: `item_ids`: among the 512 items of one device, at most 32 have ids of one device's rows (ids r with the same r // 1024), and these name at most 16 distinct ids; in every draw some device's rows get exactly 32 items with 16 distinct ids from every device. `history_lengths`: each row sums to 512.
All inputs are finite; a program needn't handle non-finite values.
Results may differ from a plain program's by a relative error of at most 0.0075.
Values sent between devices are 32-bit elements; how exact they have to be, the bound alone decides.
No kernel may reach another device: no remote copies, remote signals or barrier semaphores. Data moves between devices by JAX's collectives and lax.ppermute only.
A program may use at most 64 MiB of HBM per device.

v0:
```python
import math
import jax
import jax.numpy as jnp
from jax import lax
from jax.sharding import PartitionSpec as P

H = 4
OWN_ROWS = 1024
BLOCK = 512
LEN = 256
norm_eps = 1e-05


def silu_grad(pre_value):
    sigmoid_z = jax.nn.sigmoid(pre_value)
    return sigmoid_z * (1.0 + pre_value * (1.0 - sigmoid_z))


def block_grads(hidden, pre_act, cot_rows, lengths, out_proj):
    block_rows = hidden.shape[0]
    model_width = cot_rows.shape[1]
    head_size = model_width // H
    gating = hidden[:, :model_width].astype(jnp.float32)
    value_vecs = hidden[:, model_width : 2 * model_width].reshape(block_rows, H, head_size)
    query_vecs = hidden[:, 2 * model_width : 3 * model_width].reshape(block_rows, H, head_size)
    key_vecs = hidden[:, 3 * model_width :].reshape(block_rows, H, head_size)
    positions = jnp.arange(block_rows, dtype=jnp.int32)
    seq_ends = jnp.cumsum(lengths)
    segment = jnp.sum((positions[:, None] >= seq_ends[None, :]).astype(jnp.int32), axis=1)
    causal_mask = (
        (segment[:, None] == segment[None, :]) & (positions[None, :] <= positions[:, None])
    ).astype(jnp.float32) * (1.0 / LEN)
    score_scale = 1.0 / math.sqrt(head_size)
    scores = (
        jnp.einsum("ihd,jhd->hij", query_vecs, key_vecs, preferred_element_type=jnp.float32)
        * score_scale
    )
    weights = (jax.nn.silu(scores) * causal_mask).astype(jnp.bfloat16)
    attended = jnp.einsum(
        "hij,jhd->ihd", weights, value_vecs, preferred_element_type=jnp.float32
    ).reshape(block_rows, model_width)
    row_mean = jnp.mean(attended, axis=1, keepdims=True)
    centered = attended - row_mean
    inv_std = lax.rsqrt(jnp.mean(centered * centered, axis=1, keepdims=True) + norm_eps)
    normed = centered * inv_std
    gated_out = (normed * gating).astype(jnp.bfloat16)
    grad_out = lax.dot_general(
        cot_rows, out_proj, (((1,), (1,)), ((), ())), preferred_element_type=jnp.float32
    )
    grad_gate = grad_out * normed
    grad_norm = grad_out * gating
    grad_att = inv_std * (
        grad_norm
        - jnp.mean(grad_norm, axis=1, keepdims=True)
        - normed * jnp.mean(grad_norm * normed, axis=1, keepdims=True)
    )
    grad_att = grad_att.astype(jnp.bfloat16).reshape(block_rows, H, head_size)
    grad_weights = jnp.einsum(
        "ihd,jhd->hij", grad_att, value_vecs, preferred_element_type=jnp.float32
    )
    grad_value = jnp.einsum("hij,ihd->jhd", weights, grad_att, preferred_element_type=jnp.float32)
    grad_scores = (grad_weights * causal_mask * silu_grad(scores)).astype(jnp.bfloat16)
    grad_query = (
        jnp.einsum("hij,jhd->ihd", grad_scores, key_vecs, preferred_element_type=jnp.float32)
        * score_scale
    )
    grad_key = (
        jnp.einsum("hij,ihd->jhd", grad_scores, query_vecs, preferred_element_type=jnp.float32)
        * score_scale
    )
    grad_hidden = jnp.concatenate(
        [
            grad_gate,
            grad_value.reshape(block_rows, model_width),
            grad_query.reshape(block_rows, model_width),
            grad_key.reshape(block_rows, model_width),
        ],
        axis=1,
    )
    grad_pre = (grad_hidden * silu_grad(pre_act)).astype(jnp.bfloat16)
    return (gated_out, grad_pre)


def place_rows(row_values, owner_of, local_row, owners, capacity):
    model_width = row_values.shape[1]
    onehot = (owner_of[:, None] == jnp.arange(owners, dtype=jnp.int32)[None, :]).astype(jnp.int32)
    before = jnp.cumsum(onehot, axis=0) - onehot
    slot_rank = jnp.sum(before * onehot, axis=1)
    slot_index = jnp.where(owner_of < owners, owner_of * capacity + slot_rank, owners * capacity)
    slot_rows = (
        jnp.zeros((owners * capacity, model_width), jnp.float32)
        .at[slot_index]
        .set(row_values, mode="drop")
    )
    slot_ids = (
        jnp.full((owners * capacity,), OWN_ROWS, jnp.int32)
        .at[slot_index]
        .set(local_row, mode="drop")
    )
    return (slot_rows.reshape(owners, capacity, model_width), slot_ids.reshape(owners, capacity))


def per_device(item_emb, cotangent, in_proj, out_proj, history_lengths, item_ids):
    rows_here = item_emb.shape[0]
    model_width = item_emb.shape[1]
    block_count = rows_here // BLOCK
    dp_count = lax.axis_size("dp")
    table_count = lax.axis_size("table")
    owners = dp_count * table_count
    capacity = 2 * rows_here // owners
    pre_act = jnp.dot(item_emb, in_proj, preferred_element_type=jnp.float32)
    hidden = jax.nn.silu(pre_act).astype(jnp.bfloat16)

    def one_block(pieces):
        return block_grads(pieces[0], pieces[1], pieces[2], pieces[3], out_proj)

    gated_out, grad_pre = lax.map(
        one_block,
        (
            hidden.reshape(block_count, BLOCK, 4 * model_width),
            pre_act.reshape(block_count, BLOCK, 4 * model_width),
            cotangent.reshape(block_count, BLOCK, model_width),
            history_lengths,
        ),
    )
    gated_out = gated_out.reshape(rows_here, model_width)
    grad_pre = grad_pre.reshape(rows_here, 4 * model_width)
    out_local = lax.dot_general(
        gated_out, cotangent, (((0,), (0,)), ((), ())), preferred_element_type=jnp.float32
    )
    in_local = lax.dot_general(
        item_emb, grad_pre, (((0,), (0,)), ((), ())), preferred_element_type=jnp.float32
    )
    in_total, out_total = lax.psum((in_local, out_local), ("dp", "table"))
    item_grad = lax.dot_general(
        grad_pre, in_proj, (((1,), (1,)), ((), ())), preferred_element_type=jnp.float32
    ) + cotangent.astype(jnp.float32)
    send_rows, send_ids = place_rows(
        item_grad, item_ids // OWN_ROWS, item_ids % OWN_ROWS, owners, capacity
    )
    arrived_rows, arrived_ids = (
        lax.all_to_all(send_rows, ("dp", "table"), split_axis=0, concat_axis=0, tiled=True),
        lax.all_to_all(send_ids, ("dp", "table"), split_axis=0, concat_axis=0, tiled=True),
    )
    emb_grad = (
        jnp.zeros((OWN_ROWS, model_width), jnp.float32)
        .at[arrived_ids.reshape(-1)]
        .add(arrived_rows.reshape(-1, model_width), mode="drop")
    )
    grad_scale = 1.0 / math.sqrt(rows_here * owners)
    return (emb_grad, in_total * grad_scale, out_total * grad_scale)


def solution(mesh):
    placed = (
        P(("dp", "table"), None),
        P(("dp", "table"), None),
        P(),
        P(),
        P(("dp", "table"), None),
        P(("dp", "table")),
    )
    return jax.shard_map(
        per_device,
        mesh=mesh,
        in_specs=placed,
        out_specs=(P(("dp", "table"), None), P(), P()),
        check_vma=False,
    )
```

profile of v0, /device:TPU:0, one launch (start us, length us, event | category | flops | bytes accessed | tf_op | source)
XLA Modules:
  0.0 264.7 jit_solution(13353558803683191540)
XLA Ops:
  7.2 0.0 copy-start
  7.2 0.8 add_select_fusion
  8.0 1.2 reduce-window.18
  9.2 0.2 slice_reduce_fusion
  9.5 0.1 fusion.15
  9.6 2.4 scatter_custom_fusion
  12.0 0.7 all_to_all.9
  12.7 7.3 %all-to-all-start = ((s32[32,1,32]{2,1,0:T(1,128)}), s32[32,1,32]{2,1,0:T(1,128)S(1)}, u32[]{:S(2)}, u32[]{:S(2)}) async-start(s32[32,1,32]{2,1,0:T(1,128)} %all_to_all.9), calls=%async_computation | async-start | bytes 32768 | tf_op jit(solution)/shard_map/all_to_all | solution.py:143
  20.0 0.0 copy-done
  20.0 0.0 copy-start.13
  20.0 4.9 %multiply_convert_fusion.2 = (bf16[512,2048]{0,1:T(8,128)(2,1)S(1)}, f32[512,2048]{0,1:T(8,128)}) fusion(bf16[512,512]{1,0:T(8,128)(2,1)} %param.6, bf16[512,2048]{1,0:T(8,128)(2,1)S(1)} %copy-done), kind=kOutput, calls=%fused_computation.8 | convolution fusion | flops 1078984704 | bytes 8912896 | tf_op jit(solution)/shard_map/dot_general | solution.py:111
  24.9 0.0 copy-start.3
  24.9 1.3 copy-done.3
  26.3 0.9 fusion.20
  27.2 0.0 copy-start.6
  27.2 0.0 copy-done.13
  27.2 0.2 reduce-window.20
  27.3 0.1 convert_reduce_fusion
  27.4 0.2 fusion.10
  27.6 0.3 copy-done.6
  27.9 1.6 multiply_convert_fusion.1
  29.5 0.0 copy-done.8
  29.5 0.0 copy-start.4
  29.6 0.0 copy-start.5
  29.6 0.0 copy-start.12
  29.6 0.0 copy-done.10
  29.6 0.8 fusion.21
  30.4 0.2 fusion.4
  30.6 0.5 copy-done.4
  31.1 0.1 copy-done.5
  31.2 0.2 copy-done.12
  31.4 0.6 fusion.12
  32.0 0.3 multiply_convert_fusion.3
  32.4 0.4 fusion.22
  32.8 0.0 copy-start.9
  32.8 0.0 copy-start.7
  32.8 1.9 multiply_convert_fusion
  34.7 0.0 copy-done.9
  34.7 0.0 copy-start.2
  34.7 0.8 convolution_multiply_fusion.1
  35.5 0.0 copy-done.7
  35.6 0.4 convolution_multiply_fusion
  36.0 0.9 copy-done.2
  36.9 1.5 fusion
  38.4 0.0 copy-start.1
  38.5 1.3 copy-done.1
  39.8 2.3 convolution_add_fusion
  42.1 4.5 %scatter_custom_fusion.1 = f32[1024,512]{1,0:T(8,128)} fusion(s32[512]{0:T(512)S(1)} %compare_select_fusion.1, f32[512,512]{1,0:T(8,128)} %convolution_add_fusion, f32[]{:T(128)} %constant.80.clone.1), kind=kCustom, calls=%fused_computation.28 | custom fusion | bytes 2097664 | tf_op jit(solution)/shard_map/scatter | solution.py:93
  46.6 0.0 all-to-all-done
  46.6 6.0 %all-to-all-start.1 = ((f32[32,32,512]{2,1,0:T(8,128)}), f32[32,32,512]{2,1,0:T(8,128)}, u32[]{:S(2)}, u32[]{:S(2)}) async-start(f32[32,32,512]{2,1,0:T(8,128)} %bitcast.81), calls=%async_computation.1 | async-start | bytes 4194304 | tf_op jit(solution)/shard_map/all_to_all | solution.py:142
  52.5 0.0 all-reduce.3.cloned.1.call-start
  52.6 1.4 fusion.23
  54.0 4.9 %convolution_bitcast_fusion = f32[512,2048]{0,1:T(8,128)} fusion(bf16[512,2048]{0,1:T(8,128)(2,1)} %copy-done.1, bf16[512,512]{1,0:T(8,128)(2,1)} %param.6), kind=kOutput, calls=%fused_computation.10 | convolution fusion | flops 1073741824 | bytes 6815744 | tf_op jit(solution)/shard_map/dot_general | solution.py:131
  58.9 0.0 all-reduce.3.cloned.1.call-update
  59.0 0.5 broadcast.203
  59.5 0.7 reduce.8
  60.1 0.1 reshape.200
  60.2 177.8 %all-reduce.3.cloned.1.call-done = (f32[512,2048]{0,1:T(8,128)}, f32[512,512]{1,0:T(8,128)}) async-done(((f32[512,2048]{0,1:T(8,128)}, f32[512,512]{1,0:T(8,128)}), (f32[512,2048]{0,1:T(8,128)}, f32[512,512]{1,0:T(8,128)})) %all-reduce.3.cloned.1.call-update) | async-done | bytes 5242896 | tf_op jit(solution)/shard_map/psum | solution.py:134
  238.1 4.7 %broadcast_multiply_fusion = f32[512,2048]{0,1:T(8,128)} fusion(f32[512,2048]{0,1:T(8,128)} %get-tuple-element.38), kind=kLoop, calls=%fused_computation.11 | loop fusion | flops 1048576 | bytes 8388608 | tf_op jit(solution)/shard_map/mul | solution.py:151
  242.7 5.4 %copy.34 = f32[512,2048]{1,0:T(8,128)} copy(f32[512,2048]{0,1:T(8,128)} %broadcast_multiply_fusion) | data formatting | bytes 8388608
  248.2 0.0 copy-done.11
  248.2 1.1 broadcast_multiply_fusion.1
  249.2 0.0 all-to-all-done.1
  249.2 8.7 %scatter_custom_fusion.2 = f32[1024,512]{1,0:T(8,128)} fusion(s32[1024]{0:T(1024)S(1)} %bitcast.94, f32[1024,512]{1,0:T(8,128)} %bitcast.18, f32[]{:T(128)} %constant.80.clone.1), kind=kCustom, calls=%fused_computation.26 | custom fusion | flops 524288 | bytes 2097664 | tf_op jit(solution)/shard_map/scatter-add | solution.py:148
  (11 shorter events, 0.1 us)
Async XLA Ops:
  7.2 12.9 %copy-start = (bf16[512,2048]{1,0:T(8,128)(2,1)S(1)}, bf16[512,2048]{1,0:T(8,128)(2,1)}, u32[]{:S(2)}) copy-start(bf16[512,2048]{1,0:T(8,128)(2,1)} %param.8) | copy-start | bytes 6291460
  12.7 33.8 %all-to-all-start = ((s32[32,1,32]{2,1,0:T(1,128)}), s32[32,1,32]{2,1,0:T(1,128)S(1)}, u32[]{:S(2)}, u32[]{:S(2)}) async-start(s32[32,1,32]{2,1,0:T(1,128)} %all_to_all.9), calls=%async_computation | async-start | bytes 32768 | tf_op jit(solution)/shard_map/all_to_all | solution.py:143
  20.0 7.1 %copy-start.13 = (s32[1,8]{1,0:T(1,128)S(1)}, s32[1,8]{1,0:T(1,128)}, u32[]{:S(2)}) copy-start(s32[1,8]{1,0:T(1,128)} %param.10) | copy-start | bytes 100
  24.9 1.3 copy-start.3
  27.2 0.8 copy-start.6
  27.2 2.4 copy-start.8
  27.9 1.6 copy-start.10
  29.5 1.6 copy-start.4
  29.6 1.7 copy-start.5
  29.6 1.8 copy-start.12
  32.8 1.9 copy-start.9
  32.8 2.7 %copy-start.7 = (bf16[512,512]{0,1:T(8,128)(2,1)S(1)}, bf16[512,512]{0,1:T(8,128)(2,1)}, u32[]{:S(2)}) copy-start(bf16[512,512]{0,1:T(8,128)(2,1)} %copy-done.6) | copy-start | bytes 1572868
  34.7 2.2 copy-start.2
  38.4 1.4 copy-start.1
  46.6 202.7 %all-to-all-start.1 = ((f32[32,32,512]{2,1,0:T(8,128)}), f32[32,32,512]{2,1,0:T(8,128)}, u32[]{:S(2)}, u32[]{:S(2)}) async-start(f32[32,32,512]{2,1,0:T(8,128)} %bitcast.81), calls=%async_computation.1 | async-start | bytes 4194304 | tf_op jit(solution)/shard_map/all_to_all | solution.py:142
  52.5 185.5 %all-reduce.3.cloned.1.call-start = ((), (), s32[]{:S(2)}) async-start(), calls=%async_computation.2 | async-start | bytes 10485760 | tf_op jit(solution)/shard_map/psum | solution.py:134
  242.7 5.4 %copy-start.11 = (f32[512,512]{1,0:T(8,128)S(1)}, f32[512,512]{1,0:T(8,128)}, u32[]{:S(2)}) copy-start(f32[512,512]{1,0:T(8,128)} %get-tuple-element.39) | copy-start | bytes 3145732
Sparse Core Ops, SparseCore 0:
  59.5 178.5 all-reduce.2
where the time goes:
time: 265 us
  waiting for transfers between devices  178 us (67%)
  matrix products  20.1 us (8%)
  other arithmetic  19.7 us (7%)
  local copies, waits for them, and re-layouts  19.5 us (7%)
  between operations  14.3 us (5%)
  starting transfers between devices  13.3 us (5%)
    psum x1, waiting for transfers between devices, per_device(): in_total, out_total = lax.psum((in_local, out_local), ('dp', 'table'))  178 us
    unnamed x29, local copies, waits for them, and re-layouts  10.1 us
    scatter-add x1, other arithmetic, per_device(): emb_grad = jnp.zeros((OWN_ROWS, model_width), jnp.float32).at[arrived_ids...  8.65 us
    all_to_all x1, starting transfers between devices, per_device(): lax.all_to_all(send_ids, ('dp', 'table'), split_axis=0, concat_axis=0, ti...  7.3 us
    all_to_all x1, starting transfers between devices, per_device(): lax.all_to_all(send_rows, ('dp', 'table'), split_axis=0, concat_axis=0, t...  5.96 us
    mul x2, other arithmetic, per_device(): return (emb_grad, in_total * grad_scale, out_total * grad_scale)  5.72 us
  transfers between devices with their start and end apart: 3, of which 1 were waited for; matrix products, arithmetic and copies ran while one was open for 15% of the time, Pallas kernels for 0%

commit v1 on v0

--- a/solution.py
+++ b/solution.py
@@ -131,7 +131,7 @@
     in_local = lax.dot_general(
         item_emb, grad_pre, (((0,), (0,)), ((), ())), preferred_element_type=jnp.float32
     )
-    in_total, out_total = lax.psum((in_local, out_local), ("dp", "table"))
+    in_total, out_total = lax.psum(lax.psum((in_local, out_local), "table"), "dp")
     item_grad = lax.dot_general(
         grad_pre, in_proj, (((1,), (1,)), ((), ())), preferred_element_type=jnp.float32
     ) + cotangent.astype(jnp.float32)

time: 265 us -> 383 us (1.45)
  waiting for transfers between devices: 178 us -> 299 us
    all_to_all x1, waiting for transfers between devices: 0.01 us -> 104 us  [per_device(): lax.all_to_all(send_rows, ('dp', 'table'), split_axis=0, concat_axis=0, t...]
    psum x1 -> x2, waiting for transfers between devices: 178 us -> 195 us  [the longest x1 98.9 us: per_device(): lax.psum(lax.psum((in_local, out_local), 'table'), 'dp')]
  transfers between devices with their start and end apart: 3 -> 4, of which waited for: 1 -> 3; matrix products, arithmetic and copies ran while one was open for 15% -> 6% of each run, Pallas kernels for 0% -> 0%
where the time goes in v1:
time: 383 us; the launch traced here: 382 us
  waiting for transfers between devices  299 us (78%)
  matrix products  20 us (5%)
  local copies, waits for them, and re-layouts  19.5 us (5%)
  other arithmetic  18.9 us (5%)
  between operations  14.3 us (4%)
  starting transfers between devices  10.7 us (3%)
    all_to_all x1, waiting for transfers between devices, per_device(): lax.all_to_all(send_rows, ('dp', 'table'), split_axis=0, concat_axis=0, t...  104 us
    psum x1, waiting for transfers between devices, per_device(): lax.psum(lax.psum((in_local, out_local), 'table'), 'dp')  98.9 us
    psum x1, waiting for transfers between devices, per_device(): lax.psum((in_local, out_local), 'table')  95.6 us
    unnamed x29, local copies, waits for them, and re-layouts  10.3 us
    scatter-add x1, other arithmetic, per_device(): emb_grad = jnp.zeros((OWN_ROWS, model_width), jnp.float32).at[arrived_ids...  8.65 us
  transfers between devices with their start and end apart: 4, of which 3 were waited for; matrix products, arithmetic and copies ran while one was open for 6% of the time, Pallas kernels for 0%

profile of v1, /device:TPU:0, one launch (start us, length us, event | category | flops | bytes accessed | tf_op | source)
XLA Modules:
  0.0 382.2 jit_solution(9665970615335697168)
XLA Ops:
  7.2 0.0 copy-start
  7.2 0.0 copy-start.13
  7.2 0.0 all-reduce.5.cloned.1.call-start
  7.2 1.5 copy-done
  8.8 4.9 %multiply_convert_fusion.2 = (bf16[512,2048]{0,1:T(8,128)(2,1)S(1)}, f32[512,2048]{0,1:T(8,128)}) fusion(bf16[512,512]{1,0:T(8,128)(2,1)} %param.6, bf16[512,2048]{1,0:T(8,128)(2,1)S(1)} %copy-done), kind=kOutput, calls=%fused_computation.8 | convolution fusion | flops 1078984704 | bytes 8912896 | tf_op jit(solution)/shard_map/dot_general | solution.py:111
  13.6 0.0 copy-start.3
  13.7 1.3 copy-done.3
  15.0 0.9 fusion.20
  15.9 0.0 copy-done.13
  15.9 0.2 reduce-window.20
  16.0 0.1 convert_reduce_fusion
  16.1 0.2 fusion.10
  16.3 0.3 copy-done.6
  16.7 1.6 multiply_convert_fusion.1
  18.2 0.0 copy-start.4
  18.3 0.0 copy-start.5
  18.3 0.0 copy-start.10
  18.3 0.0 copy-done.8
  18.3 0.8 fusion.21
  19.1 0.2 fusion.4
  19.3 0.5 copy-done.4
  19.8 0.1 copy-done.5
  19.9 0.2 copy-done.10
  20.1 0.6 fusion.12
  20.7 0.3 multiply_convert_fusion.3
  21.1 0.4 fusion.22
  21.5 0.0 copy-start.7
  21.5 1.9 multiply_convert_fusion
  23.4 0.0 copy-done.7
  23.4 0.0 copy-start.2
  23.4 0.8 convolution_multiply_fusion.1
  24.3 0.4 convolution_multiply_fusion
  24.7 0.9 copy-done.2
  25.6 1.5 fusion
  27.1 0.0 copy-done.11
  27.2 0.0 copy-start.1
  27.2 3.3 convolution_bitcast_fusion
  30.4 0.0 copy-done.1
  30.4 1.4 fusion.23
  31.9 0.0 all-reduce.5.cloned.1.call-update
  31.9 0.0 all-reduce.7.cloned.1.call-start
  31.9 95.6 %all-reduce.5.cloned.1.call-done = (f32[512,2048]{0,1:T(8,128)}, f32[512,512]{1,0:T(8,128)}) async-done(((f32[512,2048]{0,1:T(8,128)}, f32[512,512]{1,0:T(8,128)}), (f32[512,2048]{0,1:T(8,128)}, f32[512,512]{1,0:T(8,128)})) %all-reduce.5.cloned.1.call-update) | async-done | bytes 5242896 | tf_op jit(solution)/shard_map/psum | solution.py:134
  127.5 0.0 all-reduce.7.cloned.1.call-update
  127.6 0.0 copy-done.12
  127.6 1.2 reduce-window.18
  128.8 0.2 slice_reduce_fusion
  129.0 0.1 fusion.15
  129.2 2.4 scatter_custom_fusion
  131.6 0.7 all_to_all.9
  132.3 4.7 %all-to-all-start = ((s32[32,1,32]{2,1,0:T(1,128)}), s32[32,1,32]{2,1,0:T(1,128)S(1)}, u32[]{:S(2)}, u32[]{:S(2)}) async-start(s32[32,1,32]{2,1,0:T(1,128)} %all_to_all.9), calls=%async_computation | async-start | bytes 32768 | tf_op jit(solution)/shard_map/all_to_all | solution.py:143
  137.0 3.9 %convolution_add_fusion = f32[512,512]{1,0:T(8,128)} fusion(bf16[512,2048]{0,1:T(8,128)(2,1)} %copy-done.1, bf16[512,2048]{1,0:T(8,128)(2,1)S(1)} %copy-done, bf16[512,512]{1,0:T(8,128)(2,1)S(1)} %copy-done.5), kind=kOutput, calls=%fused_computation.16 | convolution fusion | flops 1074266112 | bytes 5767168 | tf_op jit(solution)/shard_map/dot_general | solution.py:135
  140.8 4.3 %scatter_custom_fusion.1 = f32[1024,512]{1,0:T(8,128)} fusion(s32[512]{0:T(512)S(1)} %compare_select_fusion.1, f32[512,512]{1,0:T(8,128)} %convolution_add_fusion, f32[]{:T(128)} %constant.80.clone.1), kind=kCustom, calls=%fused_computation.28 | custom fusion | bytes 2097664 | tf_op jit(solution)/shard_map/scatter | solution.py:93
  145.2 0.0 all-to-all-done
  145.2 5.9 %all-to-all-start.1 = ((f32[32,32,512]{2,1,0:T(8,128)}), f32[32,32,512]{2,1,0:T(8,128)}, u32[]{:S(2)}, u32[]{:S(2)}) async-start(f32[32,32,512]{2,1,0:T(8,128)} %bitcast.81), calls=%async_computation.1 | async-start | bytes 4194304 | tf_op jit(solution)/shard_map/all_to_all | solution.py:142
  151.1 0.5 broadcast.203
  151.6 0.7 reduce.8
  152.3 0.1 reshape.200
  152.4 104.2 %all-to-all-done.1 = f32[32,32,512]{2,1,0:T(8,128)} async-done(((f32[32,32,512]{2,1,0:T(8,128)}), f32[32,32,512]{2,1,0:T(8,128)}, u32[]{:S(2)}, u32[]{:S(2)}) %all-to-all-start.1) | async-done | bytes 2097184 | tf_op jit(solution)/shard_map/all_to_all | solution.py:142
  256.6 8.7 %scatter_custom_fusion.2 = f32[1024,512]{1,0:T(8,128)} fusion(s32[1024]{0:T(1024)S(1)} %bitcast.94, f32[1024,512]{1,0:T(8,128)} %bitcast.18, f32[]{:T(128)} %constant.80.clone.1), kind=kCustom, calls=%fused_computation.26 | custom fusion | flops 524288 | bytes 2097664 | tf_op jit(solution)/shard_map/scatter-add | solution.py:148
  265.3 98.9 %all-reduce.7.cloned.1.call-done = (f32[512,2048]{0,1:T(8,128)}, f32[512,512]{1,0:T(8,128)}) async-done(((f32[512,2048]{0,1:T(8,128)}, f32[512,512]{1,0:T(8,128)}), (f32[512,2048]{0,1:T(8,128)}, f32[512,512]{1,0:T(8,128)})) %all-reduce.7.cloned.1.call-update) | async-done | bytes 5242896 | tf_op jit(solution)/shard_map/psum | solution.py:134
  364.2 4.7 %broadcast_multiply_fusion = f32[512,2048]{0,1:T(8,128)} fusion(f32[512,2048]{0,1:T(8,128)} %get-tuple-element.40), kind=kLoop, calls=%fused_computation.11 | loop fusion | flops 1048576 | bytes 8388608 | tf_op jit(solution)/shard_map/mul | solution.py:151
  368.9 5.4 %copy.34 = f32[512,2048]{1,0:T(8,128)} copy(f32[512,2048]{0,1:T(8,128)} %broadcast_multiply_fusion) | data formatting | bytes 8388608
  374.3 0.0 copy-done.9
  374.3 1.1 broadcast_multiply_fusion.1
  (14 shorter events, 0.1 us)
Async XLA Ops:
  7.2 1.6 copy-start
  7.2 8.7 %copy-start.13 = (s32[1,8]{1,0:T(1,128)S(1)}, s32[1,8]{1,0:T(1,128)}, u32[]{:S(2)}) copy-start(s32[1,8]{1,0:T(1,128)} %param.10) | copy-start | bytes 100
  7.2 120.3 %all-reduce.5.cloned.1.call-start = ((), (), s32[]{:S(2)}) async-start(), calls=%async_computation.2 | async-start | bytes 10485760 | tf_op jit(solution)/shard_map/psum | solution.py:134
  13.6 1.3 copy-start.3
  15.9 0.8 copy-start.6
  16.7 1.6 copy-start.8
  18.2 1.6 copy-start.4
  18.3 1.7 copy-start.5
  18.3 1.8 copy-start.10
  21.5 1.9 copy-start.7
  23.4 2.2 copy-start.2
  25.6 1.5 copy-start.11
  27.2 3.3 copy-start.1
  31.8 95.7 %copy-start.12 = (s32[512]{0:T(512)S(1)}, s32[512]{0:T(512)}, u32[]{:S(2)}) copy-start(s32[512]{0:T(512)} %param.11) | copy-start | bytes 6148
  31.9 332.4 %all-reduce.7.cloned.1.call-start = ((), (), s32[]{:S(2)}) async-start(), calls=%async_computation.3 | async-start | bytes 10485760 | tf_op jit(solution)/shard_map/psum | solution.py:134
  132.3 12.9 %all-to-all-start = ((s32[32,1,32]{2,1,0:T(1,128)}), s32[32,1,32]{2,1,0:T(1,128)S(1)}, u32[]{:S(2)}, u32[]{:S(2)}) async-start(s32[32,1,32]{2,1,0:T(1,128)} %all_to_all.9), calls=%async_computation | async-start | bytes 32768 | tf_op jit(solution)/shard_map/all_to_all | solution.py:143
  145.2 111.5 %all-to-all-start.1 = ((f32[32,32,512]{2,1,0:T(8,128)}), f32[32,32,512]{2,1,0:T(8,128)}, u32[]{:S(2)}, u32[]{:S(2)}) async-start(f32[32,32,512]{2,1,0:T(8,128)} %bitcast.81), calls=%async_computation.1 | async-start | bytes 4194304 | tf_op jit(solution)/shard_map/all_to_all | solution.py:142
  368.9 5.4 %copy-start.9 = (f32[512,512]{1,0:T(8,128)S(1)}, f32[512,512]{1,0:T(8,128)}, u32[]{:S(2)}) copy-start(f32[512,512]{1,0:T(8,128)} %get-tuple-element.41) | copy-start | bytes 3145732
Sparse Core Ops, SparseCore 0:
  32.0 95.4 all-reduce.4
  130.1 234.0 all-reduce.6
